TPU v7x, 32 devices: a whole 2x2x4 slice. The times are simulated.
32 devices in a mesh: hier: 8 (over y, x, core), col: 4 (over z).
Axes of the slice: x: 2, y: 2, z: 4, core: 2. Of those that a mesh axis runs over, the one named last changes fastest.
Arguments:
- densities: float32 [32, 2, 256, 256], P('hier', None, 'col'), may hold values from -6 to 6
- hamiltonian: float32 [256, 256], replicated, may hold values from -0.35355339 to 0.35355339, as said below
- couplings: float32 [2, 256, 256], replicated, may hold values from -0.088388348 to 0.088388348, as said below
- gamma: float32 [2], replicated, may hold values from 0.005 to 0.05
- coeff: float32 [2, 2], replicated, may hold values from -0.5 to 0.5
- node_count: int32 [8], replicated, may hold values from 2 to 4, as said below
Outputs:
- new_densities: float32 [32, 2, 256, 256], P('hier', None, 'col')
Inputs may be any that keep to these rules, and one draw needn't show every extreme that they name: `node_count`: at least one index of hier holds 4 nodes; every index holds 2 or more. `hamiltonian`: symmetric. `couplings`: each of the two matrices is symmetric.
All inputs are finite; a program needn't handle non-finite values.
Results may differ from a plain program's by a relative error of at most 0.00012.
Values sent between devices are 32-bit elements; how exact they have to be, the bound alone decides.
A program may use at most 64 MiB of HBM per device.

v0:
```python
import jax
import jax.numpy as jnp
from jax import lax
from jax.sharding import PartitionSpec as P

DEPTH2 = 2


step_size = 0.2


def passed_along(block, axis, distance):
    devices = range(lax.axis_size(axis))
    route = [(i - distance, i) for i in devices if i - distance in devices]
    return lax.ppermute(block, axis, route)


def hierarchy(node_count, device, slot):
    shards = node_count.shape[0]
    columns = jnp.arange(shards, dtype=jnp.int32)
    offsets = jnp.cumsum(node_count) - node_count
    live_total = jnp.sum(node_count) // DEPTH2 * DEPTH2

    def lookup(table, which):
        return jnp.sum(jnp.where(which[:, None] == columns[None, :], table[None, :], 0), axis=1)

    index = lookup(offsets, device) + slot
    live = (slot < lookup(node_count, device)) & (index < live_total)
    first = index // DEPTH2
    second = index % DEPTH2
    targets = (index + DEPTH2, index + 1, index - DEPTH2, index - 1)
    allowed = (
        live & (index + DEPTH2 < live_total),
        live & (second + 1 < DEPTH2),
        live & (first > 0),
        live & (second > 0),
    )
    found = []
    for target, valid in zip(targets, allowed):
        owner = jnp.sum((offsets[None, :] <= target[:, None]).astype(jnp.int32), axis=1) - 1
        within = target - lookup(offsets, owner)
        owner_count = lookup(node_count, owner)
        found.append((owner, within, valid, owner_count))
    return (live, first, second, found)


def combine(upward, downward, raise_w, lower_w, real, imag):
    rise = raise_w[:, None, None]
    fall = lower_w[:, None, None]
    part_re = rise * upward[:, 0] + fall * (real * downward[:, 0] - imag * downward[:, 1])
    part_im = rise * upward[:, 1] + fall * (real * downward[:, 1] + imag * downward[:, 0])
    return jnp.stack([part_re, part_im], axis=1)


def mixes(linked, levels, coeff, sign):
    result = []
    for mode in range(2):
        result.append(
            combine(
                linked[mode],
                linked[mode + 2],
                jnp.sqrt(levels[mode] + 1.0),
                jnp.sqrt(levels[mode]),
                coeff[mode, 0],
                sign * coeff[mode, 1],
            )
        )
    return result


def pick(wide, positions, masks):
    return [jnp.take(wide, positions[j], axis=0) * masks[j] for j in range(4)]


def tail_slots(block, start, half):
    return lax.dynamic_slice_in_dim(block, start, half, 0)


def slope(state, left_mat, right_mat, gamma, coeff, layout_info):
    alive, levels, positions, masks, tail_start = layout_info
    half = state.shape[0] // 2
    high = lax.Precision.HIGHEST
    own_cols = lax.all_to_all(state, "col", split_axis=3, concat_axis=2, tiled=True)
    lower = passed_along(
        (tail_slots(state, tail_start, half), tail_slots(own_cols, tail_start, half)), "hier", 1
    )
    upper = passed_along((state[:half], own_cols[:half]), "hier", -1)
    wide_rows = jnp.concatenate([lower[0], state, upper[0]], axis=0)
    wide_cols = jnp.concatenate([lower[1], own_cols, upper[1]], axis=0)
    rights = mixes(pick(wide_rows, positions, masks), levels, coeff, -1.0)
    lefts = mixes(pick(wide_cols, positions, masks), levels, coeff, 1.0)
    col_stack = jnp.concatenate([own_cols] + lefts, axis=2)
    right = jnp.einsum(
        "scij,jk->scik", jnp.concatenate([state] + rights, axis=3), right_mat, precision=high
    )
    left_cols = jnp.einsum("ij,scjk->scik", left_mat, col_stack, precision=high)
    left = lax.all_to_all(left_cols, "col", split_axis=2, concat_axis=3, tiled=True)
    comm = left - right
    damping = (levels[0] * gamma[0] + levels[1] * gamma[1])[:, None, None]
    out_re = comm[:, 1] - damping * state[:, 0]
    out_im = -comm[:, 0] - damping * state[:, 1]
    return jnp.stack([out_re, out_im], axis=1) * alive


def on_device(densities, hamiltonian, couplings, gamma, coeff, node_count):
    width = densities.shape[0]
    half = width // 2
    here = lax.axis_index("hier")
    device = jnp.full((width,), here, jnp.int32)
    slot = jnp.arange(width, dtype=jnp.int32)
    live, first, second, found = hierarchy(node_count, device, slot)
    own_count = jnp.sum(
        jnp.where(jnp.arange(node_count.shape[0], dtype=jnp.int32) == here, node_count, 0)
    )
    tail_start = own_count - half
    positions = []
    for o, w, v, c in found:
        place = jnp.where(
            o == here, half + w, jnp.where(o < here, w - (c - half), half + width + w)
        )
        positions.append(jnp.where(v, place, 0))
    masks = [v.astype(jnp.float32)[:, None, None, None] for o, w, v, c in found]
    levels = (first.astype(jnp.float32), second.astype(jnp.float32))
    alive = live.astype(jnp.float32)[:, None, None, None]
    layout_info = (alive, levels, positions, masks, tail_start)
    left_mat = jnp.concatenate([hamiltonian, couplings[0], couplings[1]], axis=1)
    right_mat = jnp.concatenate([hamiltonian, couplings[0], couplings[1]], axis=0)
    first_slope = slope(densities, left_mat, right_mat, gamma, coeff, layout_info)
    middle = densities + 0.5 * step_size * first_slope
    second_slope = slope(middle, left_mat, right_mat, gamma, coeff, layout_info)
    return densities + step_size * second_slope


def solution(mesh):
    placed = (P("hier", None, "col", None), P(), P(), P(), P(), P())
    return jax.shard_map(
        on_device,
        mesh=mesh,
        in_specs=placed,
        out_specs=P("hier", None, "col", None),
        check_vma=False,
    )
```

profile of v0, /device:TPU:3, one launch (start us, length us, event | category | flops | bytes accessed | tf_op | source)
XLA Modules:
  0.0 187.6 jit_solution(3273176700388385365)
XLA Ops:
  3.3 4.7 %all-to-all-start = ((f32[4,1,32768]{2,1,0:T(1,128)}), f32[4,1,32768]{2,1,0:T(1,128)S(1)}, u32[]{:S(2)}, u32[]{:S(2)}) async-start(f32[4,1,32768]{2,1,0:T(1,128)} %reshape.390), calls=%async_computation | async-start | bytes 1048576 | tf_op jit(solution)/shard_map/all_to_all | solution.py:83
  10.3 4.0 %collective-permute-start.2 = (f32[2,2,64,256]{3,2,1,0:T(8,128)S(1)}, f32[2,2,64,256]{3,2,1,0:T(8,128)S(1)}, u32[]{:S(2)}, u32[]{:S(2)}) collective-permute-start(f32[2,2,64,256]{3,2,1,0:T(8,128)S(1)} %get-tuple-element.57), channel_id=1, source_target_pairs={{0,4},{4,8},{8,12},{12,16},{16,20},{20,24},{24,28},{1,5},{5,9},{9,... | collective-permute-start | bytes 786440 | tf_op jit(solution)/shard_map/ppermute | solution.py:15
  14.2 1.9 %collective-permute-start.3 = (f32[2,2,64,256]{3,2,1,0:T(8,128)S(1)}, f32[2,2,64,256]{3,2,1,0:T(8,128)S(1)}, u32[]{:S(2)}, u32[]{:S(2)}) collective-permute-start(f32[2,2,64,256]{3,2,1,0:T(8,128)S(1)} %get-tuple-element.56), channel_id=1, source_target_pairs={{4,0},{8,4},{12,8},{16,12},{20,16},{24,20},{28,24},{5,1},{9,5},{13... | collective-permute-start | bytes 786440 | tf_op jit(solution)/shard_map/ppermute | solution.py:15
  26.1 2.0 %reduce = f32[4,32768]{1,0:T(4,128)S(1)} reduce(f32[4,1,32768]{2,1,0:T(1,128)S(1)} %all-to-all-done, f32[]{:T(128)} %broadcast.622), dimensions={1}, to_apply=%all_to_all.52.reduce_sub_computation | reduce | bytes 1048580 | tf_op jit(solution)/shard_map/all_to_all | solution.py:83
  29.8 1.9 %copy.44 = f32[4,2,64,4,64]{2,3,4,1,0:T(4,128)S(1)} copy(f32[4,2,64,4,64]{2,0,1,4,3:T(4,128)} %bitcast.69) | data formatting | bytes 1048576 | tf_op jit(solution)/shard_map/all_to_all | solution.py:83
  33.1 4.5 %collective-permute-start = (f32[2,2,256,64]{2,3,1,0:T(8,128)}, f32[2,2,256,64]{2,3,1,0:T(8,128)}, u32[]{:S(2)}, u32[]{:S(2)}) collective-permute-start(f32[2,2,256,64]{2,3,1,0:T(8,128)} %constant_dynamic-slice_fusion.2), channel_id=1, source_target_pairs={{0,4},{4,8},{8,12},{12,16},{16,20},{20,24},{24,28},{1,5},{5,9},{9,... | collective-permute-start | bytes 786440 | tf_op jit(solution)/shard_map/ppermute | solution.py:15
  37.7 2.0 %select_multiply_fusion.9 = f32[4,2,64,256]{3,2,1,0:T(8,128)} fusion(f32[4,2,64,256]{3,2,1,0:T(8,128)} %gather_fusion.6, f32[4]{0:T(128)S(1)} %get-tuple-element.73, pred[4]{0:T(512)(128)(4,1)S(1)} %get-tuple-element.68), kind=kLoop, calls=%fused_computation.82 | loop fusion | flops 262144 | bytes 1048596 | tf_op jit(solution)/shard_map/mul | solution.py:72
  43.3 1.9 %collective-permute-start.1 = (f32[2,2,256,64]{2,3,1,0:T(8,128)S(1)}, f32[2,2,256,64]{2,3,1,0:T(8,128)}, u32[]{:S(2)}, u32[]{:S(2)}) collective-permute-start(f32[2,2,256,64]{2,3,1,0:T(8,128)S(1)} %slice.195), channel_id=1, source_target_pairs={{4,0},{8,4},{12,8},{16,12},{20,16},{24,20},{28,24},{5,1},{9,5},{13... | collective-permute-start | bytes 786440 | tf_op jit(solution)/shard_map/ppermute | solution.py:15
  48.6 3.4 %collective-permute-done.1 = f32[2,2,256,64]{2,3,1,0:T(8,128)} collective-permute-done((f32[2,2,256,64]{2,3,1,0:T(8,128)S(1)}, f32[2,2,256,64]{2,3,1,0:T(8,128)}, u32[]{:S(2)}, u32[]{:S(2)}) %collective-permute-start.1) | collective-permute-done | bytes 262176 | tf_op jit(solution)/shard_map/ppermute | solution.py:15
  56.3 2.0 %select_multiply_fusion.13 = f32[4,2,256,64]{2,3,1,0:T(8,128)} fusion(f32[4,2,256,64]{2,3,1,0:T(8,128)} %gather_fusion.2, f32[4]{0:T(128)S(1)} %get-tuple-element.73, pred[4]{0:T(512)(128)(4,1)S(1)} %get-tuple-element.68), kind=kLoop, calls=%fused_computation.86 | loop fusion | flops 262144 | bytes 1048596 | tf_op jit(solution)/shard_map/mul | solution.py:72
  67.2 1.9 %reshape.392 = f32[4,1,32768]{2,1,0:T(1,128)} reshape(f32[256,4,2,64]{3,2,1,0:T(2,128)S(1)} %bitcast.65) | data formatting | bytes 1048576
  69.1 4.9 %all-to-all-start.1 = ((f32[4,1,32768]{2,1,0:T(1,128)}), f32[4,1,32768]{2,1,0:T(1,128)}, u32[]{:S(2)}, u32[]{:S(2)}) async-start(f32[4,1,32768]{2,1,0:T(1,128)} %reshape.392), calls=%async_computation.1 | async-start | bytes 1048576 | tf_op jit(solution)/shard_map/all_to_all | solution.py:97
  79.9 6.6 %all-to-all-done.1 = f32[4,1,32768]{2,1,0:T(1,128)} async-done(((f32[4,1,32768]{2,1,0:T(1,128)}), f32[4,1,32768]{2,1,0:T(1,128)}, u32[]{:S(2)}, u32[]{:S(2)}) %all-to-all-start.1) | async-done | bytes 524320 | tf_op jit(solution)/shard_map/all_to_all | solution.py:97
  86.5 3.0 %reduce.1 = f32[4,32768]{1,0:T(4,128)S(1)} reduce(f32[4,1,32768]{2,1,0:T(1,128)} %all-to-all-done.1, f32[]{:T(128)} %broadcast.622), dimensions={1}, to_apply=%all_to_all.56.reduce_sub_computation | reduce | bytes 1048580 | tf_op jit(solution)/shard_map/all_to_all | solution.py:97
  92.2 2.4 %fusion.49 = f32[4,2,64,256]{3,2,1,0:T(8,128)S(1)} fusion(f32[4,2,64,256]{3,2,1,0:T(8,128)S(1)} %all_to_all.59, f32[4,1,64,256]{3,2,1,0:T(8,128)S(1)} %copy-done.29, f32[4,1,64,256]{3,2,1,0:T(8,128)S(1)} %copy-done.28, f32[4,1,64,256]{3,2,1,0:T(8,128)} %get-tuple-element.43, f32[4,1,64,256]{3,2,1,0:T(8,128)S(1)} %copy-done.30, ...), kind=kOutput, calls=%fused_computation.59 | convolution fusion | flops 1210056704 | bytes 3407872 | tf_op jit(solution)/shard_map/scij,jk->scik/dot_general | solution.py:93
  95.6 1.9 %reshape.394 = f32[4,1,32768]{2,1,0:T(1,128)} reshape(f32[256,4,2,64]{3,2,1,0:T(2,128)S(1)} %bitcast.68) | data formatting | bytes 1048576
  97.5 3.5 %all-to-all-start.2 = ((f32[4,1,32768]{2,1,0:T(1,128)}), f32[4,1,32768]{2,1,0:T(1,128)S(1)}, u32[]{:S(2)}, u32[]{:S(2)}) async-start(f32[4,1,32768]{2,1,0:T(1,128)} %reshape.394), calls=%async_computation.2 | async-start | bytes 1048576 | tf_op jit(solution)/shard_map/all_to_all | solution.py:83
  101.1 1.9 %collective-permute-start.7 = (f32[2,2,64,256]{3,2,1,0:T(8,128)S(1)}, f32[2,2,64,256]{3,2,1,0:T(8,128)S(1)}, u32[]{:S(2)}, u32[]{:S(2)}) collective-permute-start(f32[2,2,64,256]{3,2,1,0:T(8,128)S(1)} %get-tuple-element.55), channel_id=1, source_target_pairs={{4,0},{8,4},{12,8},{16,12},{20,16},{24,20},{28,24},{5,1},{9,5},{13... | collective-permute-start | bytes 786440 | tf_op jit(solution)/shard_map/ppermute | solution.py:15
  103.0 4.5 %collective-permute-start.6 = (f32[2,2,64,256]{3,2,1,0:T(8,128)S(1)}, f32[2,2,64,256]{3,2,1,0:T(8,128)S(1)}, u32[]{:S(2)}, u32[]{:S(2)}) collective-permute-start(f32[2,2,64,256]{3,2,1,0:T(8,128)S(1)} %get-tuple-element.54), channel_id=1, source_target_pairs={{0,4},{4,8},{8,12},{12,16},{16,20},{20,24},{24,28},{1,5},{5,9},{9,... | collective-permute-start | bytes 786440 | tf_op jit(solution)/shard_map/ppermute | solution.py:15
  107.5 3.4 %collective-permute-done.7 = f32[2,2,64,256]{3,2,1,0:T(8,128)S(1)} collective-permute-done((f32[2,2,64,256]{3,2,1,0:T(8,128)S(1)}, f32[2,2,64,256]{3,2,1,0:T(8,128)S(1)}, u32[]{:S(2)}, u32[]{:S(2)}) %collective-permute-start.7) | collective-permute-done | bytes 262176 | tf_op jit(solution)/shard_map/ppermute | solution.py:15
  112.4 3.5 %all-to-all-done.2 = f32[4,1,32768]{2,1,0:T(1,128)S(1)} async-done(((f32[4,1,32768]{2,1,0:T(1,128)}), f32[4,1,32768]{2,1,0:T(1,128)S(1)}, u32[]{:S(2)}, u32[]{:S(2)}) %all-to-all-start.2) | async-done | bytes 524320 | tf_op jit(solution)/shard_map/all_to_all | solution.py:83
  115.9 2.0 %reduce.2 = f32[4,32768]{1,0:T(4,128)S(1)} reduce(f32[4,1,32768]{2,1,0:T(1,128)S(1)} %all-to-all-done.2, f32[]{:T(128)} %broadcast.622), dimensions={1}, to_apply=%all_to_all.60.reduce_sub_computation | reduce | bytes 1048580 | tf_op jit(solution)/shard_map/all_to_all | solution.py:83
  119.8 1.9 %copy.42 = f32[4,2,64,4,64]{2,3,4,1,0:T(4,128)S(1)} copy(f32[4,2,64,4,64]{2,1,0,4,3:T(2,128)} %bitcast.72) | data formatting | bytes 1048576 | tf_op jit(solution)/shard_map/all_to_all | solution.py:83
  124.8 3.7 %collective-permute-start.4 = (f32[2,2,256,64]{2,3,1,0:T(8,128)}, f32[2,2,256,64]{2,3,1,0:T(8,128)}, u32[]{:S(2)}, u32[]{:S(2)}) collective-permute-start(f32[2,2,256,64]{2,3,1,0:T(8,128)} %constant_dynamic-slice_fusion), channel_id=1, source_target_pairs={{0,4},{4,8},{8,12},{12,16},{16,20},{20,24},{24,28},{1,5},{5,9},{9,... | collective-permute-start | bytes 786440 | tf_op jit(solution)/shard_map/ppermute | solution.py:15
  128.4 2.0 %select_multiply_fusion.1 = f32[4,2,64,256]{3,2,1,0:T(8,128)} fusion(f32[4,2,64,256]{3,2,1,0:T(8,128)} %gather_fusion.14, f32[4]{0:T(128)S(1)} %get-tuple-element.73, pred[4]{0:T(512)(128)(4,1)S(1)} %get-tuple-element.68), kind=kLoop, calls=%fused_computation.74 | loop fusion | flops 262144 | bytes 1048596 | tf_op jit(solution)/shard_map/mul | solution.py:72
  134.0 1.9 %collective-permute-start.5 = (f32[2,2,256,64]{2,3,1,0:T(8,128)S(1)}, f32[2,2,256,64]{2,3,1,0:T(8,128)}, u32[]{:S(2)}, u32[]{:S(2)}) collective-permute-start(f32[2,2,256,64]{2,3,1,0:T(8,128)S(1)} %slice.226), channel_id=1, source_target_pairs={{4,0},{8,4},{12,8},{16,12},{20,16},{24,20},{28,24},{5,1},{9,5},{13... | collective-permute-start | bytes 786440 | tf_op jit(solution)/shard_map/ppermute | solution.py:15
  140.3 2.4 %collective-permute-done.5 = f32[2,2,256,64]{2,3,1,0:T(8,128)} collective-permute-done((f32[2,2,256,64]{2,3,1,0:T(8,128)S(1)}, f32[2,2,256,64]{2,3,1,0:T(8,128)}, u32[]{:S(2)}, u32[]{:S(2)}) %collective-permute-start.5) | collective-permute-done | bytes 262176 | tf_op jit(solution)/shard_map/ppermute | solution.py:15
  154.7 2.2 %fusion.40 = f32[4,2,256,64]{2,3,1,0:T(8,128)} fusion(f32[4,1,256,64]{2,3,1,0:T(8,128)S(1)} %get-tuple-element.41, f32[4,1,256,64]{2,3,1,0:T(8,128)S(1)} %get-tuple-element.40, f32[4,1,256,64]{2,3,1,0:T(8,128)S(1)} %get-tuple-element.39, f32[4,1,256,64]{2,3,1,0:T(8,128)S(1)} %get-tuple-element.38, f32[4,2,256,64]{2,3,1,0:T(8,128)S(1)} %copy-done.6, ...), kind=kOutput, calls=%fused_computation.56 | convolution fusion | flops 1209925632 | bytes 2883584 | tf_op jit(solution)/shard_map/ij,scjk->scik/dot_general | solution.py:96
  160.5 4.3 %all-to-all-start.3 = ((f32[4,1,32768]{2,1,0:T(1,128)}), f32[4,1,32768]{2,1,0:T(1,128)}, u32[]{:S(2)}, u32[]{:S(2)}) async-start(f32[4,1,32768]{2,1,0:T(1,128)} %reshape.396), calls=%async_computation.3 | async-start | bytes 1048576 | tf_op jit(solution)/shard_map/all_to_all | solution.py:97
  171.5 6.9 %all-to-all-done.3 = f32[4,1,32768]{2,1,0:T(1,128)} async-done(((f32[4,1,32768]{2,1,0:T(1,128)}), f32[4,1,32768]{2,1,0:T(1,128)}, u32[]{:S(2)}, u32[]{:S(2)}) %all-to-all-start.3) | async-done | bytes 524320 | tf_op jit(solution)/shard_map/all_to_all | solution.py:97
  178.4 3.0 %reduce.3 = f32[4,32768]{1,0:T(4,128)S(1)} reduce(f32[4,1,32768]{2,1,0:T(1,128)} %all-to-all-done.3, f32[]{:T(128)} %broadcast.622), dimensions={1}, to_apply=%all_to_all.64.reduce_sub_computation | reduce | bytes 1048580 | tf_op jit(solution)/shard_map/all_to_all | solution.py:97
  183.9 2.6 %fusion.46 = f32[4,2,64,256]{3,2,1,0:T(8,128)S(1)} fusion(f32[4,2,64,256]{3,2,1,0:T(8,128)S(1)} %all_to_all.67, f32[4,1,64,256]{3,2,1,0:T(8,128)} %get-tuple-element.37, f32[4,1,64,256]{3,2,1,0:T(8,128)S(1)} %copy-done.27, f32[4,1,64,256]{3,2,1,0:T(8,128)} %get-tuple-element.35, f32[4,1,64,256]{3,2,1,0:T(8,128)} %get-tuple-element.34, ...), kind=kOutput, calls=%fused_computation.58 | convolution fusion | flops 1210056704 | bytes 3407872 | tf_op jit(solution)/shard_map/scij,jk->scik/dot_general | solution.py:93
  (177 shorter events, 83.1 us)
Async XLA Ops:
  1.5 6.5 %copy-start.31 = (s32[8]{0:T(128)S(1)}, s32[8]{0:T(128)}, u32[]{:S(2)}) copy-start(s32[8]{0:T(128)} %param.15) | copy-start | bytes 100
  1.6 8.6 %copy-start = (f32[4,2,64,256]{3,2,1,0:T(8,128)S(1)}, f32[4,2,64,256]{3,2,1,0:T(8,128)}, u32[]{:S(2)}) copy-start(f32[4,2,64,256]{3,2,1,0:T(8,128)} %param.10) | copy-start | bytes 1572868
  3.3 15.4 %copy-start.33 = (f32[2]{0:T(128)S(1)}, f32[2]{0:T(128)}, u32[]{:S(2)}) copy-start(f32[2]{0:T(128)} %param.13) | copy-start | bytes 28
  3.3 17.9 %copy-start.20 = (f32[2,256,256]{2,1,0:T(8,128)S(1)}, f32[2,256,256]{2,1,0:T(8,128)}, u32[]{:S(2)}) copy-start(f32[2,256,256]{2,1,0:T(8,128)} %param.12) | copy-start | bytes 1572868
  3.3 22.3 %all-to-all-start = ((f32[4,1,32768]{2,1,0:T(1,128)}), f32[4,1,32768]{2,1,0:T(1,128)S(1)}, u32[]{:S(2)}, u32[]{:S(2)}) async-start(f32[4,1,32768]{2,1,0:T(1,128)} %reshape.390), calls=%async_computation | async-start | bytes 1048576 | tf_op jit(solution)/shard_map/all_to_all | solution.py:83
  10.2 11.9 %copy-start.32 = (f32[2,2]{1,0:T(2,128)S(1)}, f32[2,2]{1,0:T(2,128)}, u32[]{:S(2)}) copy-start(f32[2,2]{1,0:T(2,128)} %param.14) | copy-start | bytes 52
  10.3 13.8 %collective-permute-start.2 = (f32[2,2,64,256]{3,2,1,0:T(8,128)S(1)}, f32[2,2,64,256]{3,2,1,0:T(8,128)S(1)}, u32[]{:S(2)}, u32[]{:S(2)}) collective-permute-start(f32[2,2,64,256]{3,2,1,0:T(8,128)S(1)} %get-tuple-element.57), channel_id=1, source_target_pairs={{0,4},{4,8},{8,12},{12,16},{16,20},{20,24},{24,28},{1,5},{5,9},{9,... | collective-permute-start | bytes 786440 | tf_op jit(solution)/shard_map/ppermute | solution.py:15
  14.2 10.0 %collective-permute-start.3 = (f32[2,2,64,256]{3,2,1,0:T(8,128)S(1)}, f32[2,2,64,256]{3,2,1,0:T(8,128)S(1)}, u32[]{:S(2)}, u32[]{:S(2)}) collective-permute-start(f32[2,2,64,256]{3,2,1,0:T(8,128)S(1)} %get-tuple-element.56), channel_id=1, source_target_pairs={{4,0},{8,4},{12,8},{16,12},{20,16},{24,20},{28,24},{5,1},{9,5},{13... | collective-permute-start | bytes 786440 | tf_op jit(solution)/shard_map/ppermute | solution.py:15
  32.4 16.2 %copy-start.7 = (f32[4,2,256,64]{2,3,1,0:T(8,128)}, f32[4,2,256,64]{2,3,1,0:T(8,128)S(1)}, u32[]{:S(2)}) copy-start(f32[4,2,256,64]{2,3,1,0:T(8,128)S(1)} %all_to_all.55) | copy-start | bytes 1572868
  33.1 14.4 %collective-permute-start = (f32[2,2,256,64]{2,3,1,0:T(8,128)}, f32[2,2,256,64]{2,3,1,0:T(8,128)}, u32[]{:S(2)}, u32[]{:S(2)}) collective-permute-start(f32[2,2,256,64]{2,3,1,0:T(8,128)} %constant_dynamic-slice_fusion.2), channel_id=1, source_target_pairs={{0,4},{4,8},{8,12},{12,16},{16,20},{20,24},{24,28},{1,5},{5,9},{9,... | collective-permute-start | bytes 786440 | tf_op jit(solution)/shard_map/ppermute | solution.py:15
  41.8 3.4 %copy-start.18 = (f32[4,2,64,256]{3,2,1,0:T(8,128)S(1)}, f32[4,2,64,256]{3,2,1,0:T(8,128)}, u32[]{:S(2)}) copy-start(f32[4,2,64,256]{3,2,1,0:T(8,128)} %gather_fusion.7) | copy-start | bytes 1572868
  43.3 8.7 %collective-permute-start.1 = (f32[2,2,256,64]{2,3,1,0:T(8,128)S(1)}, f32[2,2,256,64]{2,3,1,0:T(8,128)}, u32[]{:S(2)}, u32[]{:S(2)}) collective-permute-start(f32[2,2,256,64]{2,3,1,0:T(8,128)S(1)} %slice.195), channel_id=1, source_target_pairs={{4,0},{8,4},{12,8},{16,12},{20,16},{24,20},{28,24},{5,1},{9,5},{13... | collective-permute-start | bytes 786440 | tf_op jit(solution)/shard_map/ppermute | solution.py:15
  56.3 2.0 %copy-start.5 = (f32[4,2,256,64]{2,3,1,0:T(8,128)S(1)}, f32[4,2,256,64]{2,3,1,0:T(8,128)}, u32[]{:S(2)}) copy-start(f32[4,2,256,64]{2,3,1,0:T(8,128)} %gather_fusion.3) | copy-start | bytes 1572868
  63.3 1.6 copy-start.8
  63.3 1.6 copy-start.21
  63.3 1.6 copy-start.23
  63.3 1.6 copy-start.34
  69.1 4.9 %copy-start.17 = (f32[4,2,64,256]{3,2,1,0:T(8,128)S(1)}, f32[4,2,64,256]{3,2,1,0:T(8,128)}, u32[]{:S(2)}) copy-start(f32[4,2,64,256]{3,2,1,0:T(8,128)} %gather_fusion.4) | copy-start | bytes 1572868
  69.1 17.4 %all-to-all-start.1 = ((f32[4,1,32768]{2,1,0:T(1,128)}), f32[4,1,32768]{2,1,0:T(1,128)}, u32[]{:S(2)}, u32[]{:S(2)}) async-start(f32[4,1,32768]{2,1,0:T(1,128)} %reshape.392), calls=%async_computation.1 | async-start | bytes 1048576 | tf_op jit(solution)/shard_map/all_to_all | solution.py:97
  74.2 2.6 %copy-start.11 = (f32[4,2,64,256]{3,2,1,0:T(8,128)S(1)}, f32[4,2,64,256]{3,2,1,0:T(8,128)}, u32[]{:S(2)}) copy-start(f32[4,2,64,256]{3,2,1,0:T(8,128)} %select_multiply_fusion.9) | copy-start | bytes 1572868
  74.2 2.6 %copy-start.12 = (f32[4,2,64,256]{3,2,1,0:T(8,128)S(1)}, f32[4,2,64,256]{3,2,1,0:T(8,128)}, u32[]{:S(2)}) copy-start(f32[4,2,64,256]{3,2,1,0:T(8,128)} %select_multiply_fusion.8) | copy-start | bytes 1572868
  97.5 18.4 %all-to-all-start.2 = ((f32[4,1,32768]{2,1,0:T(1,128)}), f32[4,1,32768]{2,1,0:T(1,128)S(1)}, u32[]{:S(2)}, u32[]{:S(2)}) async-start(f32[4,1,32768]{2,1,0:T(1,128)} %reshape.394), calls=%async_computation.2 | async-start | bytes 1048576 | tf_op jit(solution)/shard_map/all_to_all | solution.py:83
  101.1 9.8 %collective-permute-start.7 = (f32[2,2,64,256]{3,2,1,0:T(8,128)S(1)}, f32[2,2,64,256]{3,2,1,0:T(8,128)S(1)}, u32[]{:S(2)}, u32[]{:S(2)}) collective-permute-start(f32[2,2,64,256]{3,2,1,0:T(8,128)S(1)} %get-tuple-element.55), channel_id=1, source_target_pairs={{4,0},{8,4},{12,8},{16,12},{20,16},{24,20},{28,24},{5,1},{9,5},{13... | collective-permute-start | bytes 786440 | tf_op jit(solution)/shard_map/ppermute | solution.py:15
  103.0 7.9 %collective-permute-start.6 = (f32[2,2,64,256]{3,2,1,0:T(8,128)S(1)}, f32[2,2,64,256]{3,2,1,0:T(8,128)S(1)}, u32[]{:S(2)}, u32[]{:S(2)}) collective-permute-start(f32[2,2,64,256]{3,2,1,0:T(8,128)S(1)} %get-tuple-element.54), channel_id=1, source_target_pairs={{0,4},{4,8},{8,12},{12,16},{16,20},{20,24},{24,28},{1,5},{5,9},{9,... | collective-permute-start | bytes 786440 | tf_op jit(solution)/shard_map/ppermute | solution.py:15
  124.8 13.5 %collective-permute-start.4 = (f32[2,2,256,64]{2,3,1,0:T(8,128)}, f32[2,2,256,64]{2,3,1,0:T(8,128)}, u32[]{:S(2)}, u32[]{:S(2)}) collective-permute-start(f32[2,2,256,64]{2,3,1,0:T(8,128)} %constant_dynamic-slice_fusion), channel_id=1, source_target_pairs={{0,4},{4,8},{8,12},{12,16},{16,20},{20,24},{24,28},{1,5},{5,9},{9,... | collective-permute-start | bytes 786440 | tf_op jit(solution)/shard_map/ppermute | solution.py:15
  132.6 3.4 %copy-start.19 = (f32[4,2,64,256]{3,2,1,0:T(8,128)S(1)}, f32[4,2,64,256]{3,2,1,0:T(8,128)}, u32[]{:S(2)}) copy-start(f32[4,2,64,256]{3,2,1,0:T(8,128)} %gather_fusion.15) | copy-start | bytes 1572868
  134.0 8.7 %collective-permute-start.5 = (f32[2,2,256,64]{2,3,1,0:T(8,128)S(1)}, f32[2,2,256,64]{2,3,1,0:T(8,128)}, u32[]{:S(2)}, u32[]{:S(2)}) collective-permute-start(f32[2,2,256,64]{2,3,1,0:T(8,128)S(1)} %slice.226), channel_id=1, source_target_pairs={{4,0},{8,4},{12,8},{16,12},{20,16},{24,20},{28,24},{5,1},{9,5},{13... | collective-permute-start | bytes 786440 | tf_op jit(solution)/shard_map/ppermute | solution.py:15
  153.0 1.6 copy-start.6
  160.5 4.3 %copy-start.16 = (f32[4,2,64,256]{3,2,1,0:T(8,128)S(1)}, f32[4,2,64,256]{3,2,1,0:T(8,128)}, u32[]{:S(2)}) copy-start(f32[4,2,64,256]{3,2,1,0:T(8,128)} %gather_fusion.12) | copy-start | bytes 1572868
  160.5 17.9 %all-to-all-start.3 = ((f32[4,1,32768]{2,1,0:T(1,128)}), f32[4,1,32768]{2,1,0:T(1,128)}, u32[]{:S(2)}, u32[]{:S(2)}) async-start(f32[4,1,32768]{2,1,0:T(1,128)} %reshape.396), calls=%async_computation.3 | async-start | bytes 1048576 | tf_op jit(solution)/shard_map/all_to_all | solution.py:97
  165.7 2.5 %copy-start.9 = (f32[4,2,64,256]{3,2,1,0:T(8,128)S(1)}, f32[4,2,64,256]{3,2,1,0:T(8,128)}, u32[]{:S(2)}) copy-start(f32[4,2,64,256]{3,2,1,0:T(8,128)} %select_multiply_fusion.1) | copy-start | bytes 1572868
  165.7 2.6 %copy-start.10 = (f32[4,2,64,256]{3,2,1,0:T(8,128)S(1)}, f32[4,2,64,256]{3,2,1,0:T(8,128)}, u32[]{:S(2)}) copy-start(f32[4,2,64,256]{3,2,1,0:T(8,128)} %select_multiply_fusion) | copy-start | bytes 1572868
  (16 other events, 20.0 us)
where the time goes:
time: 189 us; the launch traced here: 188 us
  local copies, waits for them, and re-layouts  64.8 us (34%)
  starting transfers between devices  41.8 us (22%)
  other arithmetic  40.4 us (21%)
  waiting for transfers between devices  26.2 us (14%)
  matrix products  8.67 us (5%)
  between operations  5.74 us (3%)
    ppermute x8, starting transfers between devices, passed_along(): return lax.ppermute(block, axis, route)  24.4 us
    gather x16, local copies, waits for them, and re-layouts, pick(): return [jnp.take(wide, positions[j], axis=0) * masks[j] for j in range(4)]  21.4 us
    unnamed x87, local copies, waits for them, and re-layouts  20.2 us
    mul x16, other arithmetic, pick(): return [jnp.take(wide, positions[j], axis=0) * masks[j] for j in range(4)]  13.8 us
    all_to_all x2, waiting for transfers between devices, slope(): lax.all_to_all(left_cols, 'col', split_axis=2, concat_axis=3, tiled=True)  13.5 us
    add x8, other arithmetic, combine(): rise * upward[:, 0] + fall * (real * downward[:, 0] - imag * downward[:, 1])  12.2 us
    all_to_all x2, starting transfers between devices, slope(): lax.all_to_all(left_cols, 'col', split_axis=2, concat_axis=3, tiled=True)  9.21 us
    ppermute x8, waiting for transfers between devices, passed_along(): return lax.ppermute(block, axis, route)  9.18 us
  transfers between devices with their start and end apart: 12, of which 6 were waited for; matrix products, arithmetic and copies ran while one was open for 21% of the time, Pallas kernels for 0%

commit v1 on v0

v1 whole, which is shorter than its diff:
```python
import functools

import jax
import jax.numpy as jnp
from jax import lax
from jax.experimental import pallas as pl
from jax.experimental.pallas import tpu as pltpu
from jax.sharding import PartitionSpec as P

DEPTH2 = 2
MESH = pl.DeviceIdType.MESH
step_size = 0.2


def split(value):
    high = value.astype(jnp.bfloat16)
    low = (value - high.astype(jnp.float32)).astype(jnp.bfloat16)
    return high, low


def product(both, high, rhs_high, rhs_low):
    rows = high.shape[0]
    wide = jnp.dot(both, rhs_high, preferred_element_type=jnp.float32)
    rest = jnp.dot(high, rhs_low, preferred_element_type=jnp.float32)
    return wide[:rows] + (wide[rows:] + rest)


def kernel(
    shards,
    ring,
    counts,
    gamma,
    coeff,
    x_ref,
    h_ref,
    q_ref,
    out_ref,
    full,
    mid,
    right_high,
    right_low,
    left_both,
    lefts,
    rights,
    to_upper,
    to_lower,
    from_lower,
    from_upper,
    ring_send,
    ring_recv,
    hop_send,
    hop_recv,
    own_sem,
):
    slots, _, rows, order = x_ref.shape
    here = lax.axis_index("hier")
    me = lax.axis_index("col")
    reach = ring // 2
    right = (here, lax.rem(me + 1, ring))
    left = (here, lax.rem(me + ring - 1, ring))
    has_lower = here > 0
    has_upper = here < shards - 1

    barrier = pltpu.get_barrier_semaphore()
    for neighbour in (left, right):
        pl.semaphore_signal(barrier, inc=1, device_id=neighbour, device_id_type=MESH)

    @pl.when(has_lower)
    def _():
        pl.semaphore_signal(barrier, inc=1, device_id=(here - 1, me), device_id_type=MESH)

    @pl.when(has_upper)
    def _():
        pl.semaphore_signal(barrier, inc=1, device_id=(here + 1, me), device_id_type=MESH)

    pl.semaphore_wait(barrier, 2 + has_lower.astype(jnp.int32) + has_upper.astype(jnp.int32))

    def panel(origin):
        return pl.ds(pl.multiple_of(lax.rem(origin + ring, ring) * rows, rows), rows)

    def ring_copy(section, way, distance, s, origin):
        first, size = (way, 1) if 2 * distance == ring else (0, 2)
        parts = pl.ds(first, size)
        place = full.at[section, s, parts, panel(origin), :]
        if distance == 1:
            source = (x_ref if section == 0 else mid).at[s, parts]
        else:
            source = place
        return pltpu.make_async_remote_copy(
            src_ref=source,
            dst_ref=place,
            send_sem=ring_send.at[section, way, distance - 1, s],
            recv_sem=ring_recv.at[section, way, distance - 1, s],
            device_id=right if way == 0 else left,
            device_id_type=MESH,
        )

    def sent(section, way, distance, s):
        origin = me - (distance - 1) if way == 0 else me + (distance - 1)
        return ring_copy(section, way, distance, s, origin)

    def arrived(section, way, distance, s):
        origin = me - distance if way == 0 else me + distance
        return ring_copy(section, way, distance, s, origin)

    def own_copy(section, s):
        source = (x_ref if section == 0 else mid).at[s]
        return pltpu.make_async_copy(
            source, full.at[section, s, :, panel(me), :], own_sem.at[section, s]
        )

    def hop_copy(section, way):
        source, place = (to_upper, from_lower) if way == 0 else (to_lower, from_upper)
        return pltpu.make_async_remote_copy(
            src_ref=source.at[section],
            dst_ref=place.at[section],
            send_sem=hop_send.at[section, way],
            recv_sem=hop_recv.at[section, way],
            device_id=(here + 1, me) if way == 0 else (here - 1, me),
            device_id_type=MESH,
        )

    def start_slot(section, s):
        for way in range(2):
            sent(section, way, 1, s).start()
        own_copy(section, s).start()

    for s in range(slots):
        start_slot(0, s)

    for section in range(2):

        @pl.when(jnp.logical_not(has_lower))
        def _():
            from_lower[section] = jnp.zeros(from_lower.shape[1:], jnp.float32)

        @pl.when(jnp.logical_not(has_upper))
        def _():
            from_upper[section] = jnp.zeros(from_upper.shape[1:], jnp.float32)

    mine = panel(me)
    for a in range(3):
        high, low = split(h_ref[...] if a == 0 else q_ref[a - 1])
        right_high[a], right_low[a] = high, low
        high, low = split(h_ref[mine, :] if a == 0 else q_ref[a - 1, mine, :])
        left_both[a * rows : (a + 1) * rows] = high
        left_both[(3 + a) * rows : (4 + a) * rows] = low

    offset = jnp.int32(0)
    total = jnp.int32(0)
    count = jnp.int32(0)
    for i in range(shards):
        held = counts[i]
        total = total + held
        offset = offset + jnp.where(here > i, held, 0)
        count = count + jnp.where(here == i, held, 0)
    live_total = total // DEPTH2 * DEPTH2

    def number(flag):
        return jnp.where(flag, jnp.float32(1), jnp.float32(0))

    def root(value):
        return jnp.sqrt(jnp.full((1, order), value, jnp.float32))

    def levels(q):
        node = offset + q
        level = (node + DEPTH2) // DEPTH2 - 1
        return level, node - level * DEPTH2, (node >= 0) & (node < live_total)

    alive, damping = [], []
    for s in range(slots):
        zeroth, first, inside = levels(s)
        alive.append(number(inside & (s < count)))
        damping.append(
            zeroth.astype(jnp.float32) * gamma[0] + first.astype(jnp.float32) * gamma[1]
        )
    edges = range(-DEPTH2, slots + DEPTH2)
    weights = {}
    for q in edges:
        zeroth, first, inside = levels(q)
        target = number(inside)
        base = jnp.maximum(zeroth, 0).astype(jnp.float32)
        above = first.astype(jnp.float32)
        if 0 <= q + DEPTH2 < slots:
            weights[q, "up0"] = root(base + 1.0) * (target * alive[q + DEPTH2])
        if 0 <= q - DEPTH2 < slots:
            weights[q, "down0"] = root(base) * (target * alive[q - DEPTH2])
        if 0 <= q + 1 < slots:
            ok = number(first + 1 < DEPTH2)
            weights[q, "up1"] = root(above + 1.0) * (target * alive[q + 1] * ok)
        if 0 <= q - 1 < slots:
            weights[q, "down1"] = root(above) * (target * alive[q - 1])

    def gathered(q):
        total_re = total_im = None

        def plus(total, term):
            return term if total is None else total + term

        for mode, stride in ((0, DEPTH2), (1, 1)):
            a = mode + 1
            for name, m in (("up", q + stride), ("down", q - stride)):
                if not 0 <= m < slots:
                    continue
                weight = weights[q, f"{name}{mode}"]
                left_re = lefts[m, 0, a * rows : (a + 1) * rows]
                left_im = lefts[m, 1, a * rows : (a + 1) * rows]
                right_re, right_im = rights[m, 0, a], rights[m, 1, a]
                if name == "up":
                    total_re = plus(total_re, weight * (left_re - right_re))
                    total_im = plus(total_im, weight * (left_im - right_im))
                else:
                    real = weight * coeff[mode, 0]
                    imag = weight * coeff[mode, 1]
                    total_re = plus(
                        total_re, real * (left_re - right_re) - imag * (left_im + right_im)
                    )
                    total_im = plus(
                        total_im, real * (left_im - right_im) + imag * (left_re + right_re)
                    )
        return total_re, total_im

    for section in range(2):
        state = x_ref if section == 0 else mid

        high, low = split(state[...].reshape(slots * 2 * rows, order))
        both = jnp.concatenate([high, low], axis=0)
        for a in range(3):
            value = product(both, high, right_high[a], right_low[a])
            rights[:, :, a] = value.reshape(slots, 2, rows, order)

        for distance in range(1, reach + 1):
            for s in range(slots):
                for way in range(2):
                    if 2 * (distance + 1) > ring + (ring % 2 == 1):
                        continue
                    arrived(section, way, distance, s).wait_recv()
                for way in range(2):
                    if 2 * (distance + 1) > ring + (ring % 2 == 1):
                        continue
                    sent(section, way, distance + 1, s).start()

        left_high = left_both[: 3 * rows]
        for s in range(slots):
            own_copy(section, s).wait()
            for way in range(2):
                arrived(section, way, reach, s).wait_recv()
            for p in range(2):
                high, low = split(full[section, s, p])
                lefts[s, p] = product(left_both[...], left_high, high, low)

        near = {}
        for q in edges:
            if q < 0:
                low_re, low_im = gathered(q)
                to_lower[section, q + DEPTH2, 0] = low_re
                to_lower[section, q + DEPTH2, 1] = low_im
            else:
                near[q] = gathered(q)
        for j in range(DEPTH2):
            for p in range(2):
                value = None
                for q in range(DEPTH2 + j, slots + j + 1):
                    term = number(count + j == q) * near[q][p]
                    value = term if value is None else value + term
                to_upper[section, j, p] = value

        @pl.when(has_lower)
        def _():
            hop_copy(section, 1).start()

        @pl.when(has_upper)
        def _():
            hop_copy(section, 0).start()

        @pl.when(has_lower)
        def _():
            hop_copy(section, 0).wait_recv()

        @pl.when(has_upper)
        def _():
            hop_copy(section, 1).wait_recv()

        for s in range(slots):
            parts = []
            for p in range(2):
                value = lefts[s, p, :rows] - rights[s, p, 0] + near[s][p]
                if s < DEPTH2:
                    value = value + from_lower[section, s, p]
                for j in range(DEPTH2):
                    value = value + number(s == count - DEPTH2 + j) * from_upper[section, j, p]
                parts.append(value)
            keep = alive[s]
            slope_re = (parts[1] - damping[s] * state[s, 0]) * keep
            slope_im = (-parts[0] - damping[s] * state[s, 1]) * keep
            if section == 0:
                mid[s, 0] = x_ref[s, 0] + 0.5 * step_size * slope_re
                mid[s, 1] = x_ref[s, 1] + 0.5 * step_size * slope_im
                start_slot(1, s)
            else:
                out_ref[s, 0] = x_ref[s, 0] + step_size * slope_re
                out_ref[s, 1] = x_ref[s, 1] + step_size * slope_im

    for section in range(2):
        for s in range(slots):
            for distance in range(1, reach + 1):
                for way in range(2):
                    sent(section, way, distance, s).wait_send()

        @pl.when(has_lower)
        def _():
            hop_copy(section, 1).wait_send()

        @pl.when(has_upper)
        def _():
            hop_copy(section, 0).wait_send()


def solution(mesh):
    shards, ring = mesh.shape["hier"], mesh.shape["col"]

    def on_device(densities, hamiltonian, couplings, gamma, coeff, node_count):
        slots, _, rows, order = densities.shape
        f32, bf16 = jnp.float32, jnp.bfloat16
        vmem = pl.BlockSpec(memory_space=pltpu.VMEM)
        smem = pl.BlockSpec(memory_space=pltpu.SMEM)
        edge = (2, DEPTH2, 2, rows, order)
        dma = pltpu.SemaphoreType.DMA
        return pl.pallas_call(
            functools.partial(kernel, shards, ring),
            out_shape=jax.ShapeDtypeStruct(densities.shape, f32),
            in_specs=[smem] * 3 + [vmem] * 3,
            out_specs=vmem,
            scratch_shapes=[
                pltpu.VMEM((2, slots, 2, order, order), f32),
                pltpu.VMEM((slots, 2, rows, order), f32),
                pltpu.VMEM((3, order, order), bf16),
                pltpu.VMEM((3, order, order), bf16),
                pltpu.VMEM((6 * rows, order), bf16),
                pltpu.VMEM((slots, 2, 3 * rows, order), f32),
                pltpu.VMEM((slots, 2, 3, rows, order), f32),
                pltpu.VMEM(edge, f32),
                pltpu.VMEM(edge, f32),
                pltpu.VMEM(edge, f32),
                pltpu.VMEM(edge, f32),
                dma((2, 2, ring // 2, slots)),
                dma((2, 2, ring // 2, slots)),
                dma((2, 2)),
                dma((2, 2)),
                dma((2, slots)),
            ],
            compiler_params=pltpu.CompilerParams(
                collective_id=0, has_side_effects=True, vmem_limit_bytes=50 * 1024 * 1024
            ),
        )(node_count, gamma, coeff, densities, hamiltonian, couplings)

    return jax.shard_map(
        on_device,
        mesh=mesh,
        in_specs=(P("hier", None, "col", None), P(), P(), P(), P(), P()),
        out_specs=P("hier", None, "col", None),
        check_vma=False,
    )
```

time: 189 us -> 97.1 us (0.51)
  Pallas kernels: 0 us -> 91 us
  local copies, waits for them, and re-layouts: 64.8 us -> 5.82 us
  starting transfers between devices: 41.8 us -> 0 us
  other arithmetic: 40.4 us -> 0 us
  waiting for transfers between devices: 26.2 us -> 0 us
  matrix products: 8.67 us -> 0 us
  between operations: 5.74 us -> 0.02 us
    pallas_call x0 -> x1, Pallas kernels: none -> 91 us  [on_device(): pl.pallas_call(functools.partial(kernel, shards, ring), out_shape=jax.Sha...]
    ppermute x8 -> x0, starting transfers between devices: 24.4 us -> none  [passed_along(): return lax.ppermute(block, axis, route)]
    gather x16 -> x0, local copies, waits for them, and re-layouts: 21.4 us -> none  [pick(): return [jnp.take(wide, positions[j], axis=0) * masks[j] for j in range(4)]]
    all_to_all x4 -> x0, starting transfers between devices: 17.4 us -> none  [the longest x2 9.21 us: slope(): lax.all_to_all(left_cols, 'col', split_axis=2, concat_axis=3, tiled=True)]
    all_to_all x4 -> x0, waiting for transfers between devices: 17 us -> none  [the longest x2 13.5 us: slope(): lax.all_to_all(left_cols, 'col', split_axis=2, concat_axis=3, tiled=True)]
    add x11 -> x0, other arithmetic: 14.4 us -> none  [the longest x8 12.2 us: combine(): rise * upward[:, 0] + fall * (real * downward[:, 0] - imag * downward[:, 1])]
    unnamed x87 -> x13, local copies, waits for them, and re-layouts: 20.2 us -> 5.82 us
    mul x16 -> x0, other arithmetic: 13.8 us -> none  [pick(): return [jnp.take(wide, positions[j], axis=0) * masks[j] for j in range(4)]]
  transfers between devices with their start and end apart: 12 -> 0, of which waited for: 6 -> 0; matrix products, arithmetic and copies ran while one was open for 21% -> 0% of each run, Pallas kernels for 0% -> 0%
where the time goes in v1:
time: 97.1 us; the launch traced here: 96.9 us
  Pallas kernels  91 us (94%)
  local copies, waits for them, and re-layouts  5.82 us (6%)
    pallas_call x1, Pallas kernels, on_device(): pl.pallas_call(functools.partial(kernel, shards, ring), out_shape=jax.Sha...  91 us
    unnamed x13, local copies, waits for them, and re-layouts  5.82 us

profile of v1, /device:TPU:3, one launch (start us, length us, event | category | flops | bytes accessed | tf_op | source)
XLA Modules:
  0.0 96.9 jit_solution(16414768427057879871)
XLA Ops:
  0.0 0.0 copy-start
  0.0 1.0 %copy-done = f32[4,2,64,256]{3,2,1,0:T(8,128)S(1)} copy-done((f32[4,2,64,256]{3,2,1,0:T(8,128)S(1)}, f32[4,2,64,256]{3,2,1,0:T(8,128)}, u32[]{:S(2)}) %copy-start) | copy-done | bytes 524312
  1.0 0.0 copy-start.1
  1.0 1.0 %copy-done.1 = f32[2,256,256]{2,1,0:T(8,128)S(1)} copy-done((f32[2,256,256]{2,1,0:T(8,128)S(1)}, f32[2,256,256]{2,1,0:T(8,128)}, u32[]{:S(2)}) %copy-start.1) | copy-done | bytes 524312
  2.1 0.0 copy-start.2
  2.1 0.9 copy-done.2
  3.0 0.0 copy-start.3
  3.0 0.7 copy-done.3
  3.7 0.0 copy-start.4
  3.7 0.7 copy-done.4
  4.4 0.0 copy-start.5
  4.4 0.7 copy-done.5
  5.0 91.0 %shard_map.64 = f32[4,2,64,256]{3,2,1,0:T(8,128)S(1)} custom-call(s32[8]{0:T(128)S(1)} %copy-done.4, f32[2]{0:T(128)S(1)} %copy-done.5, f32[2,2]{1,0:T(2,128)S(1)} %copy-done.3, f32[4,2,64,256]{3,2,1,0:T(8,128)S(1)} %copy-done, f32[256,256]{1,0:T(8,128)S(1)} %copy-done.2, f32[2,256,256]{2,1,0:T(8,128)S(1)} %copy-done.1), custom_call_target="tpu_custom_call" | custom-call | tf_op jit(solution)/shard_map/pallas_call | solution.py:329
  96.1 0.8 copy.8
Async XLA Ops:
  0.0 1.0 %copy-start = (f32[4,2,64,256]{3,2,1,0:T(8,128)S(1)}, f32[4,2,64,256]{3,2,1,0:T(8,128)}, u32[]{:S(2)}) copy-start(f32[4,2,64,256]{3,2,1,0:T(8,128)} %x_ref.1) | copy-start | bytes 1572868
  1.0 1.0 %copy-start.1 = (f32[2,256,256]{2,1,0:T(8,128)S(1)}, f32[2,256,256]{2,1,0:T(8,128)}, u32[]{:S(2)}) copy-start(f32[2,256,256]{2,1,0:T(8,128)} %q_ref.1) | copy-start | bytes 1572868
  2.1 0.9 copy-start.2
  3.0 0.7 copy-start.3
  3.7 0.7 copy-start.4
  4.4 0.7 copy-start.5

commit v2 on v1

--- a/solution.py
+++ b/solution.py
@@ -31,10 +31,13 @@
     counts,
     gamma,
     coeff,
+    x_hbm,
+    h_hbm,
+    q_hbm,
+    out_ref,
     x_ref,
     h_ref,
     q_ref,
-    out_ref,
     full,
     mid,
     right_high,
@@ -51,8 +54,9 @@
     hop_send,
     hop_recv,
     own_sem,
+    load_sem,
 ):
-    slots, _, rows, order = x_ref.shape
+    slots, _, rows, order = x_hbm.shape
     here = lax.axis_index("hier")
     me = lax.axis_index("col")
     reach = ring // 2
@@ -61,6 +65,13 @@
     has_lower = here > 0
     has_upper = here < shards - 1
 
+    loads = [
+        pltpu.make_async_copy(source, place, load_sem.at[i])
+        for i, (source, place) in enumerate(((x_hbm, x_ref), (h_hbm, h_ref), (q_hbm, q_ref)))
+    ]
+    for load in loads:
+        load.start()
+
     barrier = pltpu.get_barrier_semaphore()
     for neighbour in (left, right):
         pl.semaphore_signal(barrier, inc=1, device_id=neighbour, device_id_type=MESH)
@@ -83,7 +94,7 @@
         parts = pl.ds(first, size)
         place = full.at[section, s, parts, panel(origin), :]
         if distance == 1:
-            source = (x_ref if section == 0 else mid).at[s, parts]
+            source = (x_hbm if section == 0 else mid).at[s, parts]
         else:
             source = place
         return pltpu.make_async_remote_copy(
@@ -104,7 +115,7 @@
         return ring_copy(section, way, distance, s, origin)
 
     def own_copy(section, s):
-        source = (x_ref if section == 0 else mid).at[s]
+        source = (x_hbm if section == 0 else mid).at[s]
         return pltpu.make_async_copy(
             source, full.at[section, s, :, panel(me), :], own_sem.at[section, s]
         )
@@ -125,7 +136,8 @@
             sent(section, way, 1, s).start()
         own_copy(section, s).start()
 
-    for s in range(slots):
+    early, late = range(DEPTH2), range(DEPTH2, slots)
+    for s in early:
         start_slot(0, s)
 
     for section in range(2):
@@ -138,6 +150,8 @@
         def _():
             from_upper[section] = jnp.zeros(from_upper.shape[1:], jnp.float32)
 
+    for load in loads:
+        load.wait()
     mine = panel(me)
     for a in range(3):
         high, low = split(h_ref[...] if a == 0 else q_ref[a - 1])
@@ -220,43 +234,44 @@
                     )
         return total_re, total_im
 
-    for section in range(2):
+    left_high = left_both[: 3 * rows]
+
+    def right_products(section, chosen):
         state = x_ref if section == 0 else mid
-
-        high, low = split(state[...].reshape(slots * 2 * rows, order))
+        first, size = chosen[0], len(chosen)
+        value = state[first : first + size].reshape(size * 2 * rows, order)
+        high, low = split(value)
         both = jnp.concatenate([high, low], axis=0)
         for a in range(3):
             value = product(both, high, right_high[a], right_low[a])
-            rights[:, :, a] = value.reshape(slots, 2, rows, order)
-
-        for distance in range(1, reach + 1):
-            for s in range(slots):
-                for way in range(2):
-                    if 2 * (distance + 1) > ring + (ring % 2 == 1):
-                        continue
-                    arrived(section, way, distance, s).wait_recv()
-                for way in range(2):
-                    if 2 * (distance + 1) > ring + (ring % 2 == 1):
-                        continue
-                    sent(section, way, distance + 1, s).start()
-
-        left_high = left_both[: 3 * rows]
-        for s in range(slots):
-            own_copy(section, s).wait()
+            rights[first : first + size, :, a] = value.reshape(size, 2, rows, order)
+
+    def forward(section, s):
+        for distance in range(1, reach):
             for way in range(2):
-                arrived(section, way, reach, s).wait_recv()
+                arrived(section, way, distance, s).wait_recv()
+            for way in range(2):
+                sent(section, way, distance + 1, s).start()
+
+    def finish(section, s):
+        own_copy(section, s).wait()
+        for way in range(2):
+            arrived(section, way, reach, s).wait_recv()
+        for p in range(2):
+            high, low = split(full[section, s, p])
+            lefts[s, p] = product(left_both[...], left_high, high, low)
+
+    def send_lower(section):
+        for q in range(-DEPTH2, 0):
+            value = gathered(q)
             for p in range(2):
-                high, low = split(full[section, s, p])
-                lefts[s, p] = product(left_both[...], left_high, high, low)
-
-        near = {}
-        for q in edges:
-            if q < 0:
-                low_re, low_im = gathered(q)
-                to_lower[section, q + DEPTH2, 0] = low_re
-                to_lower[section, q + DEPTH2, 1] = low_im
-            else:
-                near[q] = gathered(q)
+                to_lower[section, q + DEPTH2, p] = value[p]
+
+        @pl.when(has_lower)
+        def _():
+            hop_copy(section, 1).start()
+
+    def send_upper(section, near):
         for j in range(DEPTH2):
             for p in range(2):
                 value = None
@@ -265,41 +280,76 @@
                     value = term if value is None else value + term
                 to_upper[section, j, p] = value
 
+        @pl.when(has_upper)
+        def _():
+            hop_copy(section, 0).start()
+
+    def wait_upper(section):
+        @pl.when(has_upper)
+        def _():
+            hop_copy(section, 1).wait_recv()
+
+    def wait_lower(section):
         @pl.when(has_lower)
         def _():
-            hop_copy(section, 1).start()
-
-        @pl.when(has_upper)
-        def _():
-            hop_copy(section, 0).start()
-
-        @pl.when(has_lower)
-        def _():
             hop_copy(section, 0).wait_recv()
 
-        @pl.when(has_upper)
-        def _():
-            hop_copy(section, 1).wait_recv()
-
-        for s in range(slots):
-            parts = []
-            for p in range(2):
-                value = lefts[s, p, :rows] - rights[s, p, 0] + near[s][p]
-                if s < DEPTH2:
-                    value = value + from_lower[section, s, p]
-                for j in range(DEPTH2):
-                    value = value + number(s == count - DEPTH2 + j) * from_upper[section, j, p]
-                parts.append(value)
-            keep = alive[s]
-            slope_re = (parts[1] - damping[s] * state[s, 0]) * keep
-            slope_im = (-parts[0] - damping[s] * state[s, 1]) * keep
-            if section == 0:
-                mid[s, 0] = x_ref[s, 0] + 0.5 * step_size * slope_re
-                mid[s, 1] = x_ref[s, 1] + 0.5 * step_size * slope_im
-                start_slot(1, s)
-            else:
-                out_ref[s, 0] = x_ref[s, 0] + step_size * slope_re
-                out_ref[s, 1] = x_ref[s, 1] + step_size * slope_im
+    def update(section, s, near):
+        state = x_ref if section == 0 else mid
+        parts = []
+        for p in range(2):
+            value = lefts[s, p, :rows] - rights[s, p, 0] + near[s][p]
+            if s < DEPTH2:
+                value = value + from_lower[section, s, p]
+            for j in range(DEPTH2):
+                value = value + number(s == count - DEPTH2 + j) * from_upper[section, j, p]
+            parts.append(value)
+        slope_re = (parts[1] - damping[s] * state[s, 0]) * alive[s]
+        slope_im = (-parts[0] - damping[s] * state[s, 1]) * alive[s]
+        place, length = (mid, 0.5 * step_size) if section == 0 else (out_ref, step_size)
+        place[s, 0] = x_ref[s, 0] + length * slope_re
+        place[s, 1] = x_ref[s, 1] + length * slope_im
+
+    right_products(0, range(slots))
+    for i, s in enumerate(early):
+        forward(0, s)
+        if DEPTH2 + i < slots:
+            start_slot(0, DEPTH2 + i)
+    for s in range(slots):
+        if s >= 1 and s + DEPTH2 - 1 < slots:
+            forward(0, s + DEPTH2 - 1)
+        if s == DEPTH2:
+            send_lower(0)
+        finish(0, s)
+    near = {q: gathered(q) for q in range(DEPTH2, slots + DEPTH2)}
+    send_upper(0, near)
+    wait_upper(0)
+    for s in late:
+        update(0, s, near)
+        start_slot(1, s)
+    near = {q: gathered(q) for q in early}
+    for s in late:
+        forward(1, s)
+    wait_lower(0)
+    for s in early:
+        update(0, s, near)
+        start_slot(1, s)
+    right_products(1, early)
+    right_products(1, late)
+    for s in late:
+        finish(1, s)
+    for s in early:
+        forward(1, s)
+    for s in early:
+        finish(1, s)
+    send_lower(1)
+    near = {q: gathered(q) for q in range(DEPTH2, slots + DEPTH2)}
+    send_upper(1, near)
+    near.update({q: gathered(q) for q in early})
+    wait_upper(1)
+    wait_lower(1)
+    for s in range(slots):
+        update(1, s, near)
 
     for section in range(2):
         for s in range(slots):
@@ -329,9 +379,12 @@
         return pl.pallas_call(
             functools.partial(kernel, shards, ring),
             out_shape=jax.ShapeDtypeStruct(densities.shape, f32),
-            in_specs=[smem] * 3 + [vmem] * 3,
+            in_specs=[smem] * 3 + [pl.BlockSpec(memory_space=pltpu.HBM)] * 3,
             out_specs=vmem,
             scratch_shapes=[
+                pltpu.VMEM((slots, 2, rows, order), f32),
+                pltpu.VMEM((order, order), f32),
+                pltpu.VMEM((2, order, order), f32),
                 pltpu.VMEM((2, slots, 2, order, order), f32),
                 pltpu.VMEM((slots, 2, rows, order), f32),
                 pltpu.VMEM((3, order, order), bf16),
@@ -348,6 +401,7 @@
                 dma((2, 2)),
                 dma((2, 2)),
                 dma((2, slots)),
+                dma((3,)),
             ],
             compiler_params=pltpu.CompilerParams(
                 collective_id=0, has_side_effects=True, vmem_limit_bytes=50 * 1024 * 1024

time: 97.1 us -> 93.3 us (0.961)
  Pallas kernels: 91 us -> 86.5 us
    pallas_call x1, Pallas kernels: 91 us -> 86.5 us  [on_device(): pl.pallas_call(functools.partial(kernel, shards, ring), out_shape=jax.Sha...]
where the time goes in v2:
time: 93.3 us; the launch traced here: 92.3 us
  Pallas kernels  86.5 us (93%)
  local copies, waits for them, and re-layouts  5.82 us (6%)
    pallas_call x1, Pallas kernels, on_device(): pl.pallas_call(functools.partial(kernel, shards, ring), out_shape=jax.Sha...  86.5 us
    unnamed x13, local copies, waits for them, and re-layouts  5.82 us

profile of v2, /device:TPU:3, one launch (start us, length us, event | category | flops | bytes accessed | tf_op | source)
XLA Modules:
  0.0 92.3 jit_solution(3680051100173494095)
XLA Ops:
  0.0 0.0 copy-start
  0.0 1.0 %copy-done = f32[4,2,64,256]{3,2,1,0:T(8,128)S(1)} copy-done((f32[4,2,64,256]{3,2,1,0:T(8,128)S(1)}, f32[4,2,64,256]{3,2,1,0:T(8,128)}, u32[]{:S(2)}) %copy-start) | copy-done | bytes 524312
  1.0 0.0 copy-start.1
  1.0 1.0 %copy-done.1 = f32[2,256,256]{2,1,0:T(8,128)S(1)} copy-done((f32[2,256,256]{2,1,0:T(8,128)S(1)}, f32[2,256,256]{2,1,0:T(8,128)}, u32[]{:S(2)}) %copy-start.1) | copy-done | bytes 524312
  2.1 0.0 copy-start.2
  2.1 0.9 %copy-done.2 = f32[256,256]{1,0:T(8,128)S(1)} copy-done((f32[256,256]{1,0:T(8,128)S(1)}, f32[256,256]{1,0:T(8,128)}, u32[]{:S(2)}) %copy-start.2) | copy-done | bytes 262168
  3.0 0.0 copy-start.3
  3.0 0.7 copy-done.3
  3.7 0.0 copy-start.4
  3.7 0.7 copy-done.4
  4.4 0.0 copy-start.5
  4.4 0.7 copy-done.5
  5.0 86.5 %shard_map.64 = f32[4,2,64,256]{3,2,1,0:T(8,128)S(1)} custom-call(s32[8]{0:T(128)S(1)} %copy-done.4, f32[2]{0:T(128)S(1)} %copy-done.5, f32[2,2]{1,0:T(2,128)S(1)} %copy-done.3, f32[4,2,64,256]{3,2,1,0:T(8,128)S(1)} %copy-done, f32[256,256]{1,0:T(8,128)S(1)} %copy-done.2, f32[2,256,256]{2,1,0:T(8,128)S(1)} %copy-done.1), custom_call_target="tpu_custom_call" | custom-call | tf_op jit(solution)/shard_map/pallas_call | solution.py:379
  91.5 0.8 copy.8
Async XLA Ops:
  0.0 1.0 %copy-start = (f32[4,2,64,256]{3,2,1,0:T(8,128)S(1)}, f32[4,2,64,256]{3,2,1,0:T(8,128)}, u32[]{:S(2)}) copy-start(f32[4,2,64,256]{3,2,1,0:T(8,128)} %x_hbm.1) | copy-start | bytes 1572868
  1.0 1.0 %copy-start.1 = (f32[2,256,256]{2,1,0:T(8,128)S(1)}, f32[2,256,256]{2,1,0:T(8,128)}, u32[]{:S(2)}) copy-start(f32[2,256,256]{2,1,0:T(8,128)} %q_hbm.1) | copy-start | bytes 1572868
  2.1 0.9 %copy-start.2 = (f32[256,256]{1,0:T(8,128)S(1)}, f32[256,256]{1,0:T(8,128)}, u32[]{:S(2)}) copy-start(f32[256,256]{1,0:T(8,128)} %h_hbm.1) | copy-start | bytes 786436
  3.0 0.7 copy-start.3
  3.7 0.7 copy-start.4
  4.4 0.7 copy-start.5

commit v3 on v2

--- a/solution.py
+++ b/solution.py
@@ -404,7 +404,7 @@
                 dma((3,)),
             ],
             compiler_params=pltpu.CompilerParams(
-                collective_id=0, has_side_effects=True, vmem_limit_bytes=50 * 1024 * 1024
+                collective_id=0, has_side_effects=True, vmem_limit_bytes=67_043_328
             ),
         )(node_count, gamma, coeff, densities, hamiltonian, couplings)
 

time: 93.3 us -> 90.4 us (0.969)
  local copies, waits for them, and re-layouts: 5.82 us -> 1.87 us
  Pallas kernels: 86.5 us -> 87.5 us
    unnamed x13 -> x1, local copies, waits for them, and re-layouts: 5.82 us -> 1.87 us
    pallas_call x1, Pallas kernels: 86.5 us -> 87.5 us  [on_device(): pl.pallas_call(functools.partial(kernel, shards, ring), out_shape=jax.Sha...]
where the time goes in v3:
time: 90.4 us; the launch traced here: 89.4 us
  Pallas kernels  87.5 us (97%)
  local copies, waits for them, and re-layouts  1.87 us (2%)
    pallas_call x1, Pallas kernels, on_device(): pl.pallas_call(functools.partial(kernel, shards, ring), out_shape=jax.Sha...  87.5 us
    unnamed x1, local copies, waits for them, and re-layouts  1.87 us

profile of v3, /device:TPU:3, one launch (start us, length us, event | category | flops | bytes accessed | tf_op | source)
XLA Modules:
  0.0 89.4 jit_solution(12689368498538816452)
XLA Ops:
  0.0 87.5 %shard_map.64 = f32[4,2,64,256]{3,2,1,0:T(8,128)} custom-call(s32[8]{0:T(128)} %counts.1, f32[2]{0:T(128)} %gamma.1, f32[2,2]{1,0:T(2,128)} %coeff.1, f32[4,2,64,256]{3,2,1,0:T(8,128)} %x_hbm.1, f32[256,256]{1,0:T(8,128)} %h_hbm.1, f32[2,256,256]{2,1,0:T(8,128)} %q_hbm.1), custom_call_target="tpu_custom_call" | custom-call | tf_op jit(solution)/shard_map/pallas_call | solution.py:379
  87.6 1.9 %copy.8 = f32[4,2,64,256]{3,2,1,0:T(8,128)} copy(f32[4,2,64,256]{3,2,1,0:T(8,128)} %shard_map.64) | data formatting | bytes 1048576
